TPU v7x, 32 devices: a whole 2x2x4 slice. The times are simulated.
32 devices in a mesh: row: 8 (over y, x, core), col: 4 (over z).
Axes of the slice: x: 2, y: 2, z: 4, core: 2. Of those that a mesh axis runs over, the one named last changes fastest.
Arguments:
- tokens: bfloat16 [1024, 16384], P('col', 'row'), may hold values from -160 to 160
- norm_gain: bfloat16 [16384], P('row'), may hold values from 0.5 to 1.5
- gate_weight: bfloat16 [16384, 26624], P('row', 'col'), may hold values from -0.046875 to 0.046875
Outputs:
- gate_out: float32 [1024, 26624], P('row', 'col')
- token_peak: float32 [1024], P('col')
All inputs are finite; a program needn't handle non-finite values.
Results may differ from a plain program's by a relative error of at most 0.008.
Values may be sent and summed in bfloat16 or wider, within the bound.
A program may use at most 128 MiB of HBM per device.

v0:
```python
import jax
import jax.numpy as jnp
from jax import lax
from jax.sharding import PartitionSpec as P

D = 16384


def shards(tokens, norm_gain, gate_weight):
    values = tokens.astype(jnp.float32)
    gain = norm_gain.astype(jnp.float32)[None, :]
    squares = jnp.sum(values * values, axis=1)
    square_sum = lax.psum(squares, "row")
    inverse = lax.rsqrt(square_sum / D + 1e-05)
    normed = values * inverse[:, None] * gain
    token_peak = lax.pmax(jnp.max(jnp.abs(normed), axis=1), "row")
    scale = ((token_peak + 1e-06) / 448.0).astype(jnp.bfloat16)
    quant = (normed / scale.astype(jnp.float32)[:, None]).astype(jnp.bfloat16)
    quant_full, scale_full = (
        lax.all_gather(quant, "col", axis=0, tiled=True),
        lax.all_gather(scale, "col", axis=0, tiled=True),
    )
    factor = scale_full.astype(jnp.float32)
    gate_out = lax.psum_scatter(
        jnp.dot(quant_full, gate_weight, preferred_element_type=jnp.float32) * factor[:, None],
        "row",
        scatter_dimension=0,
        tiled=True,
    )
    return (gate_out, token_peak)


def solution(mesh):
    in_specs = (P("col", "row"), P("row"), P("row", "col"))
    out_specs = (P("row", "col"), P("col"))
    return jax.shard_map(shards, mesh=mesh, in_specs=in_specs, out_specs=out_specs, check_vma=False)
```

profile of v0, /device:TPU:16, one launch (start us, length us, event | category | flops | bytes accessed | tf_op | source)
XLA Modules:
  0.0 331.0 jit_solution(1611541879448605113)
XLA Ops:
  7.2 0.0 copy-start
  7.2 0.0 all-gather.3.cloned.1.call-start
  7.2 1.6 fusion
  8.8 13.7 %psum.7 = f32[256]{0:T(256)S(1)} all-reduce(f32[256]{0:T(256)S(1)} %fusion), channel_id=1, replica_groups=mesh['row'=8,'col'=4] {'row'}, use_global_device_ids=true, to_apply=%region_1.0 | all-reduce | flops 256 | bytes 2048 | tf_op jit(solution)/shard_map/psum | solution.py:13
  22.5 0.7 convert_element_type.19
  23.2 1.7 fusion.4
  24.9 11.8 %pmax.7 = f32[256]{0:T(256)S(1)} all-reduce(f32[256]{0:T(256)S(1)} %fusion.4), channel_id=1, replica_groups=mesh['row'=8,'col'=4] {'row'}, use_global_device_ids=true, to_apply=%region_3.0 | all-reduce | flops 256 | bytes 2048 | tf_op jit(solution)/shard_map/pmax | solution.py:16
  36.7 0.0 copy-start.1
  36.7 0.0 copy-done
  36.7 1.4 fusion.5
  38.1 0.0 all-gather.3.cloned.1.call-update
  38.1 0.0 reduce-scatter.2.cloned.1.call-start
  38.1 8.2 %all-gather = bf16[4,1,256]{2,1,0:T(2,128)(2,1)S(1)} all-gather(bf16[1,1,256]{2,1,0:T(2,128)(2,1)S(1)} %reshape.8), channel_id=1, replica_groups=mesh['row'=8,'col'=4] {'col'}, dimensions={0}, use_global_device_ids=true | all-gather | bytes 2560 | tf_op jit(solution)/shard_map/all_gather | solution.py:21
  46.4 70.3 %all-gather.3.cloned.1.call-done = bf16[1024,2048]{1,0:T(8,128)(2,1)} async-done(((bf16[256,2048]{1,0:T(8,128)(2,1)}), bf16[1024,2048]{1,0:T(8,128)(2,1)}) %all-gather.3.cloned.1.call-update) | async-done | bytes 4194320 | tf_op jit(solution)/shard_map/all_gather | solution.py:20
  116.7 38.0 %convolution_multiply_fusion = f32[1024,6656]{1,0:T(8,128)} fusion(bf16[1024,2048]{1,0:T(8,128)(2,1)} %all-gather.3.cloned.1.call-done, bf16[2048,6656]{1,0:T(8,128)(2,1)} %param.5, f32[1024]{0:T(1024)S(1)} %bitcast.3), kind=kOutput, calls=%fused_computation | convolution fusion | flops 27924103168 | bytes 58724352 | tf_op jit(solution)/shard_map/dot_general | solution.py:25
  154.7 0.0 copy-done.1
  154.7 0.0 reduce-scatter.2.cloned.1.call-update
  154.7 169.5 %reduce-scatter.2.cloned.1.call-done = f32[128,6656]{1,0:T(8,128)} async-done(((f32[1024,6656]{1,0:T(8,128)}), f32[128,6656]{1,0:T(8,128)}) %reduce-scatter.2.cloned.1.call-update) | async-done | bytes 3407888 | tf_op jit(solution)/shard_map/reduce_scatter | solution.py:24
  (4 shorter events, 0.0 us)
Async XLA Ops:
  7.2 29.5 %copy-start = (bf16[256,2048]{1,0:T(8,128)(2,1)S(1)}, bf16[256,2048]{1,0:T(8,128)(2,1)}, u32[]{:S(2)}) copy-start(bf16[256,2048]{1,0:T(8,128)(2,1)} %param.3) | copy-start | bytes 3145732
  7.2 109.5 %all-gather.3.cloned.1.call-start = ((), (), s32[]{:S(2)}) async-start(), calls=%async_computation.1 | async-start | bytes 5242880 | tf_op jit(solution)/shard_map/all_gather | solution.py:20
  36.7 118.0 %copy-start.1 = (f32[256]{0:T(256)}, f32[256]{0:T(256)S(1)}, u32[]{:S(2)}) copy-start(f32[256]{0:T(256)S(1)} %pmax.7) | copy-start | bytes 3076
  38.1 286.1 %reduce-scatter.2.cloned.1.call-start = ((), (), s32[]{:S(2)}) async-start(), calls=%async_computation.2 | async-start | bytes 30670848 | tf_op jit(solution)/shard_map/reduce_scatter | solution.py:24
Sparse Core Ops, SparseCore 0:
  38.2 78.4 all-gather.2
  154.8 169.2 reduce-scatter.1
where the time goes:
time: 333 us; the launch traced here: 331 us
  waiting for transfers between devices  240 us (72%)
  matrix products  38 us (11%)
  blocking collectives  33.7 us (10%)
  between operations  14.1 us (4%)
  other arithmetic  5.36 us (2%)
    reduce_scatter x1, waiting for transfers between devices, shards(): lax.psum_scatter(jnp.dot(quant_full, gate_weight, preferred_element_type=...  169 us
    all_gather x1, waiting for transfers between devices, shards(): lax.all_gather(quant, 'col', axis=0, tiled=True)  70.3 us
    dot_general x1, matrix products, shards(): jnp.dot(quant_full, gate_weight, preferred_element_type=jnp.float32)  38 us
    psum x1, blocking collectives, shards(): square_sum = lax.psum(squares, 'row')  13.7 us
    pmax x1, blocking collectives, shards(): token_peak = lax.pmax(jnp.max(jnp.abs(normed), axis=1), 'row')  11.8 us
    all_gather x1, blocking collectives, shards(): lax.all_gather(scale, 'col', axis=0, tiled=True)  8.24 us
  transfers between devices with their start and end apart: 2, of which 2 were waited for; matrix products, arithmetic and copies ran while one was open for 0% of the time, Pallas kernels for 0%

commit v1 on v0

v1 whole, which is shorter than its diff:
```python
import functools

import jax
import jax.numpy as jnp
from jax import lax
from jax.experimental import pallas as pl
from jax.experimental.pallas import tpu as pltpu
from jax.sharding import PartitionSpec as P

MESH = pl.DeviceIdType.MESH
D1 = 1
D2 = 2
ROWS = 32


def kernel(R, C, NC, w, B, K, tok_ref, gain_ref, wgt_ref, out_ref, peak_ref,
           wv, x, xg, sq, mx, own, psend, precv, cha, chb, outbuf, fac, stsrc, statc, statb,
           tok_sem, w_sem, zr_send, zl_send, z_recv, psend_sem, precv_sem,
           ca_send, ca_recv, cb_send, cb_recv, out_sem, sc_send, sc_recv, sb_send, sb_recv):
    r = lax.axis_index("row")
    c = lax.axis_index("col")
    n_chips = R // 2
    half_ring = n_chips // 2
    chip = r // 2
    core = r % 2
    partner = r + 1 - 2 * core
    H = B // 2
    Q = H // 2
    items = C * NC
    slots = own.shape[0]

    def ring_pos(i):
        return jnp.where(i % 2 == 0, i // 2, 2 * half_ring - 1 - i // 2)

    def ring_chip(q):
        return jnp.where(q < half_ring, 2 * q, 2 * (2 * half_ring - 1 - q) + 1)

    pos = ring_pos(chip)
    nxt = ring_chip((pos + 1) % n_chips) * 2 + core
    prv = ring_chip((pos + n_chips - 1) % n_chips) * 2 + core

    near = jnp.minimum(c, C - 1 - c)

    def block_of(i):
        step = (i + 1) // 2
        close = jnp.where(i % 2 == 1, c - step, c + step)
        far = jnp.where(c <= C - 1 - c, c + (i - near), c - (i - near))
        return jnp.where(i <= 2 * near, close, far)

    tok_copy = pltpu.make_async_copy(tok_ref, x.at[c], tok_sem)
    tok_copy.start()

    def w_copy(n):
        cols = pl.ds(pl.multiple_of(n * w, w), w)
        return pltpu.make_async_copy(wgt_ref.at[:, cols], wv.at[n], w_sem.at[n])

    barrier = pltpu.get_barrier_semaphore()
    for o in range(1, R):
        pl.semaphore_signal(barrier, inc=1, device_id={"row": (r + o) % R}, device_id_type=MESH)

    @pl.when(c > 0)
    def _():
        pl.semaphore_signal(barrier, inc=1, device_id={"col": c - 1}, device_id_type=MESH)

    @pl.when(c < C - 1)
    def _():
        pl.semaphore_signal(barrier, inc=1, device_id={"col": c + 1}, device_id_type=MESH)

    @pl.loop(0, NC)
    def _(n):
        w_copy(n).start()

    neighbours = jnp.where(c > 0, 1, 0) + jnp.where(c < C - 1, 1, 0)
    pl.semaphore_wait(barrier, R - 1 + neighbours)

    def z_right(src, b, s):
        return pltpu.make_async_remote_copy(
            src_ref=src, dst_ref=x.at[b], send_sem=zr_send.at[s], recv_sem=z_recv.at[b],
            device_id={"col": c + 1}, device_id_type=MESH)

    def z_left(src, b, s):
        return pltpu.make_async_remote_copy(
            src_ref=src, dst_ref=x.at[b], send_sem=zl_send.at[s], recv_sem=z_recv.at[b],
            device_id={"col": c - 1}, device_id_type=MESH)

    @pl.when(c < C - 1)
    def _():
        z_right(tok_ref, c, 0).start()

    @pl.when(c > 0)
    def _():
        z_left(tok_ref, c, 0).start()

    tok_copy.wait()

    def part_copy(g):
        return pltpu.make_async_remote_copy(
            src_ref=psend.at[g], dst_ref=precv.at[g], send_sem=psend_sem.at[g], recv_sem=precv_sem.at[g],
            device_id={"row": partner}, device_id_type=MESH)

    def chain_copy(buf, send, recv, g, to):
        return pltpu.make_async_remote_copy(
            src_ref=buf.at[g], dst_ref=buf.at[g], send_sem=send.at[g], recv_sem=recv.at[g],
            device_id={"row": to}, device_id_type=MESH)

    def statc_copy(o):
        return pltpu.make_async_remote_copy(
            src_ref=stsrc.at[0], dst_ref=statc.at[r], send_sem=sc_send.at[o], recv_sem=sc_recv.at[r],
            device_id={"row": (r + o) % R}, device_id_type=MESH)

    def statb_copy(i, k, to):
        return pltpu.make_async_remote_copy(
            src_ref=stsrc.at[i], dst_ref=statb.at[r], send_sem=sb_send.at[i, k], recv_sem=sb_recv.at[r],
            device_id={"row": to}, device_id_type=MESH)

    def stat_wait(buf, sem, o):
        q = (r + o) % R
        pltpu.make_async_remote_copy(
            src_ref=stsrc.at[0], dst_ref=buf.at[q], send_sem=sc_send.at[0], recv_sem=sem.at[q],
            device_id={"row": q}, device_id_type=MESH).wait_recv()

    def out_copy(h, n):
        rows = pl.ds(h * Q, Q)
        cols = pl.ds(pl.multiple_of(n * w, w), w)
        return pltpu.make_async_copy(outbuf.at[rows, cols], out_ref.at[rows, cols], out_sem.at[h, n])

    def start_block(i):
        b = block_of(i)

        @pl.when((i > 0) & (c - i >= 0))
        def _():
            z_right(x.at[c - i], c - i, 0).wait_recv()

            @pl.when(c < C - 1)
            def _():
                z_right(x.at[c - i], c - i, i).start()

        @pl.when((i > 0) & (c + i <= C - 1))
        def _():
            z_left(x.at[c + i], c + i, 0).wait_recv()

            @pl.when(c > 0)
            def _():
                z_left(x.at[c + i], c + i, i).start()

        gain = gain_ref[...].astype(jnp.float32)

        @pl.loop(0, B // ROWS)
        def _(q):
            rows = pl.ds(pl.multiple_of(q * ROWS, ROWS), ROWS)
            total = jnp.zeros((ROWS, 128), jnp.float32)
            top = jnp.zeros((ROWS, 128), jnp.float32)
            for j in range(K // 128):
                cols = slice(j * 128, (j + 1) * 128)
                v = x[b, rows, cols].astype(jnp.float32)
                y = v * gain[:, cols]
                total = total + v * v
                top = jnp.maximum(top, jnp.abs(y))
                xg[rows, cols] = y.astype(jnp.bfloat16)
            sq[rows, :] = total
            mx[rows, :] = top

        s = jnp.sum(sq[...].T, axis=0, keepdims=True)
        m = jnp.max(mx[...].T, axis=0, keepdims=True)
        line = lax.broadcasted_iota(jnp.int32, (8, B), 0)
        both = jnp.where(line < 4, jnp.broadcast_to(s, (8, B)), jnp.broadcast_to(m, (8, B)))
        stsrc[i] = both

        @pl.when(i == 0)
        def _():
            statc[r] = both
            for o in range(1, R):
                statc_copy(o).start()

        @pl.when(chip == b)
        def _():
            statb[r] = both

        for k in range(2):
            @pl.when(r != 2 * b + k)
            def _():
                statb_copy(i, k, 2 * b + k).start()

    def totals(buf):
        s = buf[0, 0:4, :]
        m = buf[0, 4:8, :]
        for q in range(1, R):
            s = s + buf[q, 0:4, :]
            m = jnp.maximum(m, buf[q, 4:8, :])
        inverse = lax.rsqrt(s / (K * R) + 1e-05)
        return inverse, m * inverse

    def make_factor():
        for o in range(1, R):
            stat_wait(statb, sb_recv, o)
        inverse, peak = totals(statb)
        scale = ((peak + 1e-06) / 448.0).astype(jnp.bfloat16).astype(jnp.float32)
        factor = (inverse / scale) * scale
        mine = jnp.where(core == 0, factor[0:1, :H], factor[0:1, H:])
        fac[...] = jnp.broadcast_to(mine, (H, H)).T

    def chain(g, lag, h, buf, send, recv, to):
        i = g // NC
        n = g % NC
        b_pos = ring_pos(block_of(i))
        stage = (pos + n_chips - b_pos - 1) % n_chips if h == 0 else (b_pos + n_chips - pos - 1) % n_chips

        @pl.when(stage == lag)
        def _():
            rows = slice(h * Q, (h + 1) * Q)
            v = own[g % slots, rows, :]
            if lag > 0:
                chain_copy(buf, send, recv, g, to).wait_recv()
                v = v + buf[g].astype(jnp.float32)
            if lag < n_chips - 1:
                buf[g] = v.astype(jnp.bfloat16)
                chain_copy(buf, send, recv, g, to).start()
            else:
                if h == 0:
                    @pl.when(n == 0)
                    def _():
                        make_factor()
                f = fac[rows, 0:1]
                cols = pl.ds(pl.multiple_of(n * w, w), w)
                outbuf[rows, cols] = v * f
                out_copy(h, n).start()

    @pl.loop(0, items + D1 + (n_chips - 1) * D2)
    def _(t):
        @pl.when(t < items)
        def _():
            i = t // NC
            n = t % NC

            @pl.when(n == 0)
            def _():
                start_block(i)

            @pl.when(i == 0)
            def _():
                w_copy(n).wait()

            product = jnp.dot(xg[...], wv[n], preferred_element_type=jnp.float32)
            own[t % slots] = jnp.where(core == 0, product[:H], product[H:])
            psend[t] = jnp.where(core == 0, product[H:], product[:H]).astype(jnp.bfloat16)
            part_copy(t).start()

        g0 = t - D1

        @pl.when((g0 >= 0) & (g0 < items))
        def _():
            part_copy(g0).wait_recv()
            own[g0 % slots] = own[g0 % slots] + precv[g0].astype(jnp.float32)

        for lag in range(n_chips):
            g = t - D1 - lag * D2

            @pl.when((g >= 0) & (g < items))
            def _():
                chain(g, lag, 0, cha, ca_send, ca_recv, nxt)
                chain(g, lag, 1, chb, cb_send, cb_recv, prv)

    for o in range(1, R):
        stat_wait(statc, sc_recv, o)
    _, peak = totals(statc)
    peak_ref[...] = peak[0:1, :]

    @pl.loop(0, items)
    def _(g):
        part_copy(g).wait_send()
        mine = block_of(g // NC) == chip

        @pl.when(jnp.logical_not(mine))
        def _():
            chain_copy(cha, ca_send, ca_recv, g, nxt).wait_send()
            chain_copy(chb, cb_send, cb_recv, g, prv).wait_send()

    for s in range(C - 1):
        @pl.when((c < C - 1) & (c - s >= 0))
        def _():
            z_right(tok_ref, c, s).wait_send()

        @pl.when((c > 0) & (c + s <= C - 1))
        def _():
            z_left(tok_ref, c, s).wait_send()

    for o in range(1, R):
        statc_copy(o).wait_send()
    for i in range(C):
        b = block_of(i)
        for k in range(2):
            @pl.when(r != 2 * b + k)
            def _():
                statb_copy(i, k, 2 * b + k).wait_send()

    @pl.loop(0, NC)
    def _(n):
        out_copy(0, n).wait()
        out_copy(1, n).wait()


def shards(R, C, tokens, norm_gain, gate_weight):
    B, K = tokens.shape
    F = gate_weight.shape[1]
    w = max(v for v in range(128, 513, 128) if F % v == 0)
    NC = F // w
    H = B // 2
    n_chips = R // 2
    assert R == 2 * C and n_chips % 2 == 0
    items = C * NC
    slots = D1 + (n_chips - 1) * D2 + 1
    dma = pltpu.SemaphoreType.DMA
    out, peak = pl.pallas_call(
        functools.partial(kernel, R, C, NC, w, B, K),
        out_shape=(
            jax.ShapeDtypeStruct((H, F), jnp.float32),
            jax.ShapeDtypeStruct((1, B), jnp.float32),
        ),
        in_specs=[
            pl.BlockSpec(memory_space=pl.ANY),
            pl.BlockSpec(memory_space=pltpu.VMEM),
            pl.BlockSpec(memory_space=pl.ANY),
        ],
        out_specs=(
            pl.BlockSpec(memory_space=pl.ANY),
            pl.BlockSpec(memory_space=pltpu.VMEM),
        ),
        scratch_shapes=[
            pltpu.VMEM((NC, K, w), jnp.bfloat16),
            pltpu.VMEM((C, B, K), jnp.bfloat16),
            pltpu.VMEM((B, K), jnp.bfloat16),
            pltpu.VMEM((B, 128), jnp.float32),
            pltpu.VMEM((B, 128), jnp.float32),
            pltpu.VMEM((slots, H, w), jnp.float32),
            pltpu.VMEM((items, H, w), jnp.bfloat16),
            pltpu.VMEM((items, H, w), jnp.bfloat16),
            pltpu.VMEM((items, H // 2, w), jnp.bfloat16),
            pltpu.VMEM((items, H // 2, w), jnp.bfloat16),
            pltpu.VMEM((H, F), jnp.float32),
            pltpu.VMEM((H, H), jnp.float32),
            pltpu.VMEM((C, 8, B), jnp.float32),
            pltpu.VMEM((R, 8, B), jnp.float32),
            pltpu.VMEM((R, 8, B), jnp.float32),
            dma,
            dma((NC,)),
            dma((C,)),
            dma((C,)),
            dma((C,)),
            dma((items,)),
            dma((items,)),
            dma((items,)),
            dma((items,)),
            dma((items,)),
            dma((items,)),
            dma((2, NC)),
            dma((R,)),
            dma((R,)),
            dma((C, 2)),
            dma((R,)),
        ],
        compiler_params=pltpu.CompilerParams(
            collective_id=0, has_side_effects=True, vmem_limit_bytes=67043328
        ),
    )(tokens, norm_gain.reshape(1, K), gate_weight)
    return out, peak.reshape(B)


def solution(mesh):
    in_specs = (P("col", "row"), P("row"), P("row", "col"))
    out_specs = (P("row", "col"), P("col"))
    f = functools.partial(shards, mesh.shape["row"], mesh.shape["col"])
    return jax.shard_map(f, mesh=mesh, in_specs=in_specs, out_specs=out_specs, check_vma=False)
```

time: 333 us -> 127 us (0.38)
  waiting for transfers between devices: 240 us -> 0 us
  Pallas kernels: 0 us -> 121 us
  matrix products: 38 us -> 0 us
  blocking collectives: 33.7 us -> 0 us
  between operations: 14.1 us -> 0.65 us
  local copies, waits for them, and re-layouts: 0.01 us -> 5.82 us
  other arithmetic: 5.36 us -> 0 us
    reduce_scatter x1 -> x0, waiting for transfers between devices: 169 us -> none  [shards(): lax.psum_scatter(jnp.dot(quant_full, gate_weight, preferred_element_type=...]
    pallas_call x0 -> x1, Pallas kernels: none -> 121 us  [shards(): pl.pallas_call(functools.partial(kernel, R, C, NC, w, B, K), out_shape=(j...]
    all_gather x1 -> x0, waiting for transfers between devices: 70.3 us -> none  [shards(): lax.all_gather(quant, 'col', axis=0, tiled=True)]
    dot_general x1 -> x0, matrix products: 38 us -> none  [shards(): jnp.dot(quant_full, gate_weight, preferred_element_type=jnp.float32)]
    psum x1 -> x0, blocking collectives: 13.7 us -> none  [shards(): square_sum = lax.psum(squares, 'row')]
    pmax x1 -> x0, blocking collectives: 11.8 us -> none  [shards(): token_peak = lax.pmax(jnp.max(jnp.abs(normed), axis=1), 'row')]
    all_gather x1 -> x0, blocking collectives: 8.24 us -> none  [shards(): lax.all_gather(scale, 'col', axis=0, tiled=True)]
    unnamed x5 -> x4, local copies, waits for them, and re-layouts: 0.01 us -> 4.53 us
  transfers between devices with their start and end apart: 2 -> 0, of which waited for: 2 -> 0; matrix products, arithmetic and copies ran while one was open for 0% -> 0% of each run, Pallas kernels for 0% -> 0%
where the time goes in v1:
time: 127 us
  Pallas kernels  121 us (95%)
  local copies, waits for them, and re-layouts  5.82 us (5%)
    pallas_call x1, Pallas kernels, shards(): pl.pallas_call(functools.partial(kernel, R, C, NC, w, B, K), out_shape=(j...  121 us
    unnamed x4, local copies, waits for them, and re-layouts  4.53 us

profile of v1, /device:TPU:16, one launch (start us, length us, event | category | flops | bytes accessed | tf_op | source)
XLA Modules:
  0.0 127.2 jit_solution(5214807250217236117)
XLA Ops:
  0.6 1.3 %reshape.10.gain_ref = bf16[1,2048]{1,0:T(2,128)(2,1)} reshape(bf16[2048]{0:T(1024)(128)(2,1)} %param.4) | data formatting | bytes 8192 | tf_op jit(solution)/shard_map/reshape | solution.py:364
  1.9 120.7 %shard_map.50 = (f32[128,6656]{1,0:T(8,128)}, f32[1,256]{1,0:T(1,128)}) custom-call(bf16[256,2048]{1,0:T(8,128)(2,1)} %tok_ref.1, bf16[1,2048]{1,0:T(2,128)(2,1)} %reshape.10.gain_ref, bf16[2048,6656]{1,0:T(8,128)(2,1)} %wgt_ref.1), custom_call_target="tpu_custom_call" | custom-call | tf_op jit(solution)/shard_map/pallas_call | solution.py:313
  122.6 0.0 copy-start
  122.7 4.0 %copy.7 = f32[128,6656]{1,0:T(8,128)} copy(f32[128,6656]{1,0:T(8,128)} %get-tuple-element.8) | data formatting | bytes 6815744
  126.6 0.0 copy-done
  126.6 0.6 copy.8
Async XLA Ops:
  122.6 4.0 %copy-start = (f32[1,256]{1,0:T(1,128)S(1)}, f32[1,256]{1,0:T(1,128)}, u32[]{:S(2)}) copy-start(f32[1,256]{1,0:T(1,128)} %get-tuple-element.5) | copy-start | bytes 3076

commit v2 on v1

--- a/solution.py
+++ b/solution.py
@@ -9,8 +9,12 @@
 
 MESH = pl.DeviceIdType.MESH
 D1 = 1
-D2 = 2
+D2 = 3
 ROWS = 32
+
+
+def lag_step(NC, n_chips):
+    return min(D2, (NC - D1) // (n_chips - 1))
 
 
 def kernel(R, C, NC, w, B, K, tok_ref, gain_ref, wgt_ref, out_ref, peak_ref,
@@ -28,6 +32,8 @@
     Q = H // 2
     items = C * NC
     slots = own.shape[0]
+    d2 = lag_step(NC, n_chips)
+    last = D1 + (n_chips - 1) * d2
 
     def ring_pos(i):
         return jnp.where(i % 2 == 0, i // 2, 2 * half_ring - 1 - i // 2)
@@ -199,16 +205,11 @@
         mine = jnp.where(core == 0, factor[0:1, :H], factor[0:1, H:])
         fac[...] = jnp.broadcast_to(mine, (H, H)).T
 
-    def chain(g, lag, h, buf, send, recv, to):
-        i = g // NC
-        n = g % NC
-        b_pos = ring_pos(block_of(i))
-        stage = (pos + n_chips - b_pos - 1) % n_chips if h == 0 else (b_pos + n_chips - pos - 1) % n_chips
-
+    def chain(stage, g, n, slot, lag, h, buf, send, recv, to):
         @pl.when(stage == lag)
         def _():
             rows = slice(h * Q, (h + 1) * Q)
-            v = own[g % slots, rows, :]
+            v = own[slot, rows, :]
             if lag > 0:
                 chain_copy(buf, send, recv, g, to).wait_recv()
                 v = v + buf[g].astype(jnp.float32)
@@ -225,40 +226,59 @@
                 outbuf[rows, cols] = v * f
                 out_copy(h, n).start()
 
-    @pl.loop(0, items + D1 + (n_chips - 1) * D2)
-    def _(t):
-        @pl.when(t < items)
-        def _():
-            i = t // NC
-            n = t % NC
-
-            @pl.when(n == 0)
-            def _():
-                start_block(i)
-
-            @pl.when(i == 0)
-            def _():
-                w_copy(n).wait()
-
-            product = jnp.dot(xg[...], wv[n], preferred_element_type=jnp.float32)
-            own[t % slots] = jnp.where(core == 0, product[:H], product[H:])
-            psend[t] = jnp.where(core == 0, product[H:], product[:H]).astype(jnp.bfloat16)
-            part_copy(t).start()
-
-        g0 = t - D1
-
-        @pl.when((g0 >= 0) & (g0 < items))
-        def _():
-            part_copy(g0).wait_recv()
-            own[g0 % slots] = own[g0 % slots] + precv[g0].astype(jnp.float32)
-
-        for lag in range(n_chips):
-            g = t - D1 - lag * D2
-
-            @pl.when((g >= 0) & (g < items))
-            def _():
-                chain(g, lag, 0, cha, ca_send, ca_recv, nxt)
-                chain(g, lag, 1, chb, cb_send, cb_recv, prv)
+    def stages(i):
+        ahead = pos + n_chips - ring_pos(block_of(i)) - 1
+        after = 2 * n_chips - 2 - ahead
+        wrap = lambda v: jnp.where(v >= n_chips, v - n_chips, v)
+        return wrap(ahead), wrap(after)
+
+    @pl.loop(0, C + 1)
+    def _(i):
+        live = i < C
+        now_a, now_b = stages(jnp.minimum(i, C - 1))
+        old_a, old_b = stages(jnp.maximum(i - 1, 0))
+        now_a = jnp.where(live, now_a, -1)
+        now_b = jnp.where(live, now_b, -1)
+        old_a = jnp.where(i > 0, old_a, -1)
+        old_b = jnp.where(i > 0, old_b, -1)
+        base = i * NC
+
+        @pl.when(live)
+        def _():
+            start_block(i)
+
+        @pl.loop(0, jnp.where(live, NC, last))
+        def _(n):
+            t = base + n
+
+            @pl.when(live)
+            def _():
+                @pl.when(i == 0)
+                def _():
+                    w_copy(n).wait()
+
+                slot = lax.rem(t, slots)
+                product = jnp.dot(xg[...], wv[n], preferred_element_type=jnp.float32)
+                own[slot] = jnp.where(core == 0, product[:H], product[H:])
+                psend[t] = jnp.where(core == 0, product[H:], product[:H]).astype(jnp.bfloat16)
+                part_copy(t).start()
+
+            g0 = t - D1
+
+            @pl.when((g0 >= 0) & (g0 < items))
+            def _():
+                part_copy(g0).wait_recv()
+                slot = lax.rem(g0, slots)
+                own[slot] = own[slot] + precv[g0].astype(jnp.float32)
+
+            for lag in range(n_chips):
+                off = D1 + lag * d2
+                fresh = n >= off
+                g = jnp.maximum(t - off, 0)
+                m = jnp.where(fresh, n - off, n - off + NC)
+                slot = lax.rem(g, slots)
+                chain(jnp.where(fresh, now_a, old_a), g, m, slot, lag, 0, cha, ca_send, ca_recv, nxt)
+                chain(jnp.where(fresh, now_b, old_b), g, m, slot, lag, 1, chb, cb_send, cb_recv, prv)
 
     for o in range(1, R):
         stat_wait(statc, sc_recv, o)
@@ -308,7 +328,9 @@
     n_chips = R // 2
     assert R == 2 * C and n_chips % 2 == 0
     items = C * NC
-    slots = D1 + (n_chips - 1) * D2 + 1
+    slots = 1
+    while slots < D1 + (n_chips - 1) * lag_step(NC, n_chips) + 1:
+        slots *= 2
     dma = pltpu.SemaphoreType.DMA
     out, peak = pl.pallas_call(
         functools.partial(kernel, R, C, NC, w, B, K),

time: 127 us -> 126 us (level)
  Pallas kernels: 121 us -> 119 us
where the time goes in v2:
time: 126 us
  Pallas kernels  119 us (94%)
  local copies, waits for them, and re-layouts  5.82 us (5%)
    pallas_call x1, Pallas kernels, shards(): pl.pallas_call(functools.partial(kernel, R, C, NC, w, B, K), out_shape=(j...  119 us
    unnamed x4, local copies, waits for them, and re-layouts  4.53 us

profile of v2, /device:TPU:16, one launch (start us, length us, event | category | flops | bytes accessed | tf_op | source)
XLA Modules:
  0.0 125.9 jit_solution(2338266472792780029)
XLA Ops:
  0.6 1.3 %reshape.10.gain_ref = bf16[1,2048]{1,0:T(2,128)(2,1)} reshape(bf16[2048]{0:T(1024)(128)(2,1)} %param.4) | data formatting | bytes 8192 | tf_op jit(solution)/shard_map/reshape | solution.py:386
  1.9 119.5 %shard_map.50 = (f32[128,6656]{1,0:T(8,128)}, f32[1,256]{1,0:T(1,128)}) custom-call(bf16[256,2048]{1,0:T(8,128)(2,1)} %tok_ref.1, bf16[1,2048]{1,0:T(2,128)(2,1)} %reshape.10.gain_ref, bf16[2048,6656]{1,0:T(8,128)(2,1)} %wgt_ref.1), custom_call_target="tpu_custom_call" | custom-call | tf_op jit(solution)/shard_map/pallas_call | solution.py:335
  121.4 0.0 copy-start
  121.4 4.0 %copy.7 = f32[128,6656]{1,0:T(8,128)} copy(f32[128,6656]{1,0:T(8,128)} %get-tuple-element.8) | data formatting | bytes 6815744
  125.4 0.0 copy-done
  125.4 0.6 copy.8
Async XLA Ops:
  121.4 4.0 %copy-start = (f32[1,256]{1,0:T(1,128)S(1)}, f32[1,256]{1,0:T(1,128)}, u32[]{:S(2)}) copy-start(f32[1,256]{1,0:T(1,128)} %get-tuple-element.5) | copy-start | bytes 3076
